TPU v7x, 256 devices: a whole 4x4x8 slice. The times are simulated.
256 devices in a mesh: batch: 32 (over z, x), tensor: 8 (over y, core).
Axes of the slice: x: 4, y: 4, z: 8, core: 2. Of those that a mesh axis runs over, the one named last changes fastest.
Arguments:
- tokens: bfloat16 [8192, 4096], P(('batch', 'tensor')), may hold values from -6 to 6
- norm_gain: float32 [4096], replicated, may hold values from 0.1 to 1.9
- w_query: bfloat16 [4096, 4096], P(None, 'tensor'), may hold values from -0.09375 to 0.09375
- w_key: bfloat16 [4096, 1024], P(None, 'tensor'), may hold values from -0.25 to 0.25
- w_value: bfloat16 [4096, 1024], P(None, 'tensor'), may hold values from -0.09375 to 0.09375
- w_out: bfloat16 [4096, 4096], P('tensor'), may hold values from -0.25 to 0.25
- prefix_keys: bfloat16 [16384, 1024], P('batch', 'tensor'), may hold values from -6 to 6
- prefix_values: bfloat16 [16384, 1024], P('batch', 'tensor'), may hold values from -6 to 6
- cache_keys: bfloat16 [147456, 1024], P('batch', 'tensor'), may hold values from -160 to 160
- cache_values: bfloat16 [147456, 1024], P('batch', 'tensor'), may hold values from -6 to 6
- cache_lengths: int32 [128], replicated, may hold values from 128 to 2048, as said below
- prefix_used: int32 [128], P('batch'), may hold values from 4096 to 16384
- parents: int32 [128, 64], P('batch'), may hold values from 0 to 62, as said below
- accepted_index: int32 [128, 8], P('batch'), may hold values from 0 to 63, as said below
Outputs:
- mixed_output: bfloat16 [8192, 4096], P(('batch', 'tensor'))
- accepted_keys: bfloat16 [128, 8, 1024], P('batch', None, 'tensor')
- accepted_values: bfloat16 [128, 8, 1024], P('batch', None, 'tensor')
Inputs may be any that keep to these rules, and one draw needn't show every extreme that they name: `cache_lengths`: within each aligned group of 4 requests at most 2 have more than 256 cached tokens; in the first group exactly that many do, and some request has exactly 2048. parents[r, 0] = 0; for i >= 1, parents[r, i] lies between max(0, i - 8) and i - 1. `accepted_index`: each row lists 8 tree positions, each the parent of the next, ending at a position of 32 or more; where the root is reached the row repeats 0 at its front.
All inputs are finite; a program needn't handle non-finite values.
Results may differ from a plain program's by a relative error of at most 0.015.
The roundings to bfloat16 on the way count: a program that leaves them out, or rounds other values in their place, can miss the bound.
Values may be sent and summed in bfloat16 or wider, within the bound.
A program may use at most 192 MiB of HBM per device.

v0:
```python
import jax
import jax.numpy as jnp
from jax import lax
from jax.sharding import PartitionSpec as P

HD = 128
NEG_FILL = -1e30
HIGHEST = lax.Precision.HIGHEST


def rms_normed(tokens, norm_gain):
    values = tokens.astype(jnp.float32)
    factor = lax.rsqrt(jnp.mean(values * values, axis=-1, keepdims=True) + 1e-05)
    return (values * factor * norm_gain).astype(jnp.bfloat16)


def ancestor_table(parents):
    node_count = parents.shape[-1]
    column = jnp.arange(node_count, dtype=jnp.int32)
    linked = (parents[..., None] == column).astype(jnp.float32)
    itself = (column[:, None] == column[None, :]).astype(jnp.float32)
    ancestry = jnp.minimum(linked + itself, 1.0)
    for repeat in range(node_count.bit_length()):
        ancestry = jnp.minimum(
            jnp.einsum("rij,rjk->rik", ancestry, ancestry, precision=HIGHEST), 1.0
        )
    return ancestry


def rotate(values, positions):
    half_width = values.shape[-1] // 2
    frequency = 10000.0 ** (-jnp.arange(half_width, dtype=jnp.float32) / half_width)
    angles = positions.astype(jnp.float32)[:, None] * frequency[None, :]
    cosine = jnp.cos(angles)[:, None, :]
    sine_table = jnp.sin(angles)[:, None, :]
    first_half = values[..., :half_width]
    second_half = values[..., half_width:]
    return jnp.concatenate(
        [
            first_half * cosine - second_half * sine_table,
            second_half * cosine + first_half * sine_table,
        ],
        axis=-1,
    )


def absorb(carry, scores, visible, apply_values):
    running_max, running_sum, running_out = carry
    masked = jnp.where(visible, scores, NEG_FILL)
    new_max = jnp.maximum(running_max, jnp.max(masked, axis=-1))
    weights = jnp.where(visible, jnp.exp(masked - new_max[..., None]), 0.0)
    factor = jnp.exp(running_max - new_max)
    new_sum = running_sum * factor + jnp.sum(weights, axis=-1)
    new_out = running_out * factor[..., None] + apply_values(weights.astype(jnp.bfloat16))
    return (new_max, new_sum, new_out)


def combine(first_part, second_part):
    joint_max = jnp.maximum(first_part[0], second_part[0])
    first_factor = jnp.exp(first_part[0] - joint_max)
    second_factor = jnp.exp(second_part[0] - joint_max)
    joint_sum = first_part[1] * first_factor + second_part[1] * second_factor
    joint_out = first_part[2] * first_factor[..., None] + second_part[2] * second_factor[..., None]
    return (joint_max, joint_sum, joint_out)


def empty_partials(leading, head_size):
    return (
        jnp.full(leading, NEG_FILL, jnp.float32),
        jnp.zeros(leading, jnp.float32),
        jnp.zeros(leading + (head_size,), jnp.float32),
    )


def cache_partials(queries, all_keys, all_values, lower_slot, upper_slot, score_scale):
    capacity = all_keys.shape[0]
    block_size = min(512, capacity)
    kv_local = queries.shape[1]
    head_size = queries.shape[3]

    def one_request(request_items):
        request_query, lower_bound, upper_bound = request_items
        blocks = (upper_bound - lower_bound + block_size - 1) // block_size

        def block_step(block_index, carry):
            block_begin = lower_bound + block_index * block_size
            start = jnp.clip(block_begin, 0, capacity - block_size)
            block_keys = lax.dynamic_slice_in_dim(all_keys, start, block_size, 0).reshape(
                block_size, kv_local, head_size
            )
            block_values = lax.dynamic_slice_in_dim(all_values, start, block_size, 0).reshape(
                block_size, kv_local, head_size
            )
            slot_ids = start + jnp.arange(block_size, dtype=jnp.int32)
            visible = (slot_ids >= block_begin) & (
                slot_ids < jnp.minimum(upper_bound, block_begin + block_size)
            )
            scores = (
                jnp.einsum(
                    "hqd,khd->hqk", request_query, block_keys, preferred_element_type=jnp.float32
                )
                * score_scale
            )
            return absorb(
                carry,
                scores,
                visible[None, None, :],
                lambda rounded: jnp.einsum(
                    "hqk,khd->hqd", rounded, block_values, preferred_element_type=jnp.float32
                ),
            )

        start_carry = empty_partials(request_query.shape[:2], head_size)
        return lax.fori_loop(0, blocks, block_step, start_carry)

    return lax.map(one_request, (queries, lower_slot, upper_slot))


def body(
    tokens,
    norm_gain,
    w_query,
    w_key,
    w_value,
    w_out,
    prefix_keys,
    prefix_values,
    cache_keys,
    cache_values,
    cache_lengths,
    prefix_used,
    parents,
    accepted_index,
):
    req_count, tree_size = parents.shape
    head_size = HD
    query_cols = w_query.shape[1]
    key_cols = w_key.shape[1]
    kv_local = key_cols // head_size
    group_size = query_cols // key_cols
    query_rows = tree_size * group_size
    score_scale = head_size ** (-0.5)
    normed = rms_normed(tokens, norm_gain)
    piece = lax.all_gather(normed, "tensor", axis=0, tiled=True)
    projected = jnp.concatenate(
        [
            jnp.dot(piece, w_query, preferred_element_type=jnp.float32),
            jnp.dot(piece, w_key, preferred_element_type=jnp.float32),
            jnp.dot(piece, w_value, preferred_element_type=jnp.float32),
        ],
        axis=1,
    )
    group_index = lax.axis_index("batch")
    own_lengths = lax.dynamic_slice_in_dim(cache_lengths, group_index * req_count, req_count)
    ancestry = ancestor_table(parents)
    tree_depth = (jnp.sum(ancestry, axis=-1) - 1.0).astype(jnp.int32)
    position = ((prefix_used + own_lengths)[:, None] + tree_depth).reshape(req_count * tree_size)
    queries = rotate(
        projected[:, :query_cols].reshape(-1, kv_local * group_size, head_size), position
    ).astype(jnp.bfloat16)
    queries = queries.reshape(req_count, tree_size, kv_local, group_size, head_size).transpose(
        0, 2, 1, 3, 4
    )
    queries = queries.reshape(req_count, kv_local, query_rows, head_size)
    new_keys = rotate(
        projected[:, query_cols : query_cols + key_cols].reshape(-1, kv_local, head_size), position
    ).astype(jnp.bfloat16)
    new_keys = new_keys.reshape(req_count, tree_size, key_cols)
    new_values = (
        projected[:, query_cols + key_cols :]
        .astype(jnp.bfloat16)
        .reshape(req_count, tree_size, key_cols)
    )
    accepted_keys = jnp.take_along_axis(new_keys, accepted_index[:, :, None], axis=1)
    accepted_values = jnp.take_along_axis(new_values, accepted_index[:, :, None], axis=1)
    tree_keys = new_keys.reshape(req_count, tree_size, kv_local, head_size)
    tree_values = new_values.reshape(req_count, tree_size, kv_local, head_size)
    tree_scores = (
        jnp.einsum("rhqd,rkhd->rhqk", queries, tree_keys, preferred_element_type=jnp.float32)
        * score_scale
    )
    tree_visible = jnp.repeat(ancestry > 0.5, group_size, axis=1)[:, None]
    tree_part = absorb(
        empty_partials((req_count, kv_local, query_rows), head_size),
        tree_scores,
        tree_visible,
        lambda rounded: jnp.einsum(
            "rhqk,rkhd->rhqd", rounded, tree_values, preferred_element_type=jnp.float32
        ),
    )
    own_offsets = jnp.cumsum(own_lengths) - own_lengths
    cache_part = cache_partials(
        queries, cache_keys, cache_values, own_offsets, own_offsets + own_lengths, score_scale
    )
    local_part = combine(tree_part, cache_part)
    piece_keys = lax.all_gather(prefix_keys, "batch", axis=0, tiled=True)
    piece_values = lax.all_gather(prefix_values, "batch", axis=0, tiled=True)
    row_count = piece_keys.shape[0]
    shaped_keys = piece_keys.reshape(row_count, kv_local, head_size)
    shaped_values = piece_values.reshape(row_count, kv_local, head_size)
    slot_ids = jnp.arange(row_count, dtype=jnp.int32)
    visible = (slot_ids[None, :] < prefix_used[:, None])[:, None, None, :]
    scores = (
        jnp.einsum("rhqd,khd->rhqk", queries, shaped_keys, preferred_element_type=jnp.float32)
        * score_scale
    )
    folded = absorb(
        local_part,
        scores,
        visible,
        lambda rounded: jnp.einsum(
            "rhqk,khd->rhqd", rounded, shaped_values, preferred_element_type=jnp.float32
        ),
    )
    attended = (folded[2] / folded[1][..., None]).astype(jnp.bfloat16)
    attended = attended.reshape(req_count, kv_local, tree_size, group_size, head_size).transpose(
        0, 2, 1, 3, 4
    )
    attended = attended.reshape(req_count * tree_size, query_cols)
    mixed_rows = lax.psum_scatter(
        jnp.dot(attended, w_out, preferred_element_type=jnp.float32).astype(jnp.bfloat16),
        "tensor",
        scatter_dimension=0,
        tiled=True,
    )
    return (mixed_rows, accepted_keys, accepted_values)


def solution(mesh):
    in_specs = (
        P(("batch", "tensor"), None),
        P(),
        P(None, "tensor"),
        P(None, "tensor"),
        P(None, "tensor"),
        P("tensor", None),
        P("batch", "tensor"),
        P("batch", "tensor"),
        P("batch", "tensor"),
        P("batch", "tensor"),
        P(),
        P("batch"),
        P("batch", None),
        P("batch", None),
    )
    out_specs = (
        P(("batch", "tensor"), None),
        P("batch", None, "tensor"),
        P("batch", None, "tensor"),
    )
    return jax.shard_map(body, mesh=mesh, in_specs=in_specs, out_specs=out_specs, check_vma=False)
```

profile of v0, /device:TPU:4, one launch (start us, length us, event | category | flops | bytes accessed | tf_op | source)
XLA Modules:
  0.0 278.1 jit_solution(979624814477540230)
XLA Ops:
  7.2 1.2 fusion.52
  8.4 1.8 fusion.54
  10.3 0.7 all-gather.6.cloned.1.call-update
  11.8 0.8 iota_compare_fusion
  12.6 0.8 dynamic-slice_add_fusion
  13.6 0.7 bitcast_subtract_fusion
  14.3 1.0 convolution_minimum_fusion.6
  18.2 23.1 %all-gather.4.cloned.1.call-done = bf16[256,4096]{1,0:T(8,128)(2,1)} async-done(((bf16[32,4096]{1,0:T(8,128)(2,1)}), bf16[256,4096]{1,0:T(8,128)(2,1)}) %all-gather.4.cloned.1.call-update) | async-done | bytes 2097168 | tf_op jit(solution)/shard_map/all_gather | solution.py:144
  41.3 4.1 %fusion.85 = f32[256,512]{1,0:T(8,128)S(1)} fusion(bf16[256,4096]{1,0:T(8,128)(2,1)} %all-gather.4.cloned.1.call-done, bf16[4096,512]{1,0:T(8,128)(2,1)} %param.22), kind=kOutput, calls=%fused_computation.133 | convolution fusion | flops 1073741824 | bytes 6815744 | tf_op jit(solution)/shard_map/dot_general | solution.py:147
  46.0 0.9 pad_maximum_fusion.1
  46.9 44.6 %while.69 = (s32[]{:T(128)}, f32[4,1,256]{2,1,0:T(1,128)S(1)}, f32[4,1,256]{2,1,0:T(1,128)S(1)}, f32[4,1,256,128]{3,2,1,0:T(8,128)}, s32[4]{0:T(128)S(1)}, /*ind...) while((s32[]{:T(128)}, f32[4,1,256]{2,1,0:T(1,128)S(1)}, ...), condition=%wide.region_9.10_spmd, body=%wide.region_4.9_spmd.sunk | while | flops 68356632 | bytes 2712316 | solution.py:116
  49.6 0.9 dynamic-slice_bitcast_fusion.3
  50.5 4.0 %while.70 = (s32[]{:T(128)}, f32[1,256]{1,0:T(1,128)S(1)}, f32[1,256]{1,0:T(1,128)S(1)}, f32[1,256,128]{2,1,0:T(8,128)S(1)}, s32[]{:T(128)}, /*index=5*/s32[]{:T...) while((s32[]{:T(128)}, f32[1,256]{1,0:T(1,128)S(1)}, ...), condition=%wide.region_8.8_spmd, body=%wide.region_5.7_spmd.sunk | while | flops 68356616 | bytes 2181353 | solution.py:114
  51.8 1.2 fusion.117
  53.2 1.3 fusion.119
  57.7 0.9 dynamic-slice_bitcast_fusion.3
  58.6 16.0 %while.70 = (s32[]{:T(128)}, f32[1,256]{1,0:T(1,128)S(1)}, f32[1,256]{1,0:T(1,128)S(1)}, f32[1,256,128]{2,1,0:T(8,128)S(1)}, s32[]{:T(128)}, /*index=5*/s32[]{:T...) while((s32[]{:T(128)}, f32[1,256]{1,0:T(1,128)S(1)}, ...), condition=%wide.region_8.8_spmd, body=%wide.region_5.7_spmd.sunk | while | flops 68356616 | bytes 2181353 | solution.py:114
  59.9 1.2 fusion.117
  61.2 1.3 fusion.119
  63.9 1.2 fusion.117
  65.2 1.3 fusion.119
  67.9 1.2 fusion.117
  69.2 1.3 fusion.119
  71.9 1.2 fusion.117
  73.2 1.3 fusion.119
  77.8 0.9 dynamic-slice_bitcast_fusion.3
  78.7 4.0 %while.70 = (s32[]{:T(128)}, f32[1,256]{1,0:T(1,128)S(1)}, f32[1,256]{1,0:T(1,128)S(1)}, f32[1,256,128]{2,1,0:T(8,128)S(1)}, s32[]{:T(128)}, /*index=5*/s32[]{:T...) while((s32[]{:T(128)}, f32[1,256]{1,0:T(1,128)S(1)}, ...), condition=%wide.region_8.8_spmd, body=%wide.region_5.7_spmd.sunk | while | flops 68356616 | bytes 2181353 | solution.py:114
  80.0 1.2 fusion.117
  81.3 1.3 fusion.119
  85.9 0.9 dynamic-slice_bitcast_fusion.3
  86.8 4.0 %while.70 = (s32[]{:T(128)}, f32[1,256]{1,0:T(1,128)S(1)}, f32[1,256]{1,0:T(1,128)S(1)}, f32[1,256,128]{2,1,0:T(8,128)S(1)}, s32[]{:T(128)}, /*index=5*/s32[]{:T...) while((s32[]{:T(128)}, f32[1,256]{1,0:T(1,128)S(1)}, ...), condition=%wide.region_8.8_spmd, body=%wide.region_5.7_spmd.sunk | while | flops 68356616 | bytes 2181353 | solution.py:114
  88.1 1.2 fusion.117
  89.4 1.3 fusion.119
  91.5 0.8 convolution_bitcast_fusion.1
  92.3 0.9 fusion.68
  93.3 1.5 copy.30
  94.8 1.5 copy.29
  96.3 1.0 pad_maximum_fusion.2
  97.8 1.3 fusion.84
  100.0 2.6 convolution_convert_fusion.1
  102.5 22.0 %all-gather.6.cloned.1.call-done = bf16[16384,128]{1,0:T(8,128)(2,1)} async-done(((bf16[512,128]{1,0:T(8,128)(2,1)}), bf16[16384,128]{1,0:T(8,128)(2,1)}) %all-gather.6.cloned.1.call-update) | async-done | bytes 4194320 | tf_op jit(solution)/shard_map/all_gather | solution.py:196
  124.5 27.2 %fusion.17 = (f32[4,256]{1,0:T(4,128)S(1)}, f32[4,256,16384]{2,1,0:T(8,128)}) fusion(pred[4,16384]{1,0:T(4,128)(4,1)S(1)} %iota_compare_fusion, bf16[16384,128]{1,0:T(8,128)(2,1)} %all-gather.6.cloned.1.call-done, bf16[4,256,64]{2,1,0:T(8,128)(2,1)} %bitcast.194, bf16[4,256,64]{2,1,0:T(8,128)(2,1)S(1)} %bitcast.191), kind=kOutput, calls=%fused_computation.30 | convolution fusion | flops 4345822208 | bytes 71634944 | tf_op jit(solution)/shard_map/rhqd,khd->rhqk/dot_general | solution.py:204
  151.8 24.3 %fusion.18 = f32[4,256]{1,0:T(4,128)S(1)} fusion(f32[4,256,16384]{2,1,0:T(8,128)} %get-tuple-element.336, f32[4,256]{1,0:T(4,128)S(1)} %get-tuple-element.337, pred[4,16384]{1,0:T(4,128)(4,1)S(1)} %iota_compare_fusion), kind=kLoop, calls=%fused_computation.31 | loop fusion | flops 83885056 | bytes 67182592 | tf_op jit(solution)/shard_map/reduce_sum | solution.py:53
  176.2 1.0 fusion.45
  177.3 28.4 %all-gather.8.cloned.1.call-done = bf16[16384,128]{1,0:T(8,128)(2,1)} async-done(((bf16[512,128]{1,0:T(8,128)(2,1)}), bf16[16384,128]{1,0:T(8,128)(2,1)}) %all-gather.8.cloned.1.call-update) | async-done | bytes 4194320 | tf_op jit(solution)/shard_map/all_gather | solution.py:197
  205.7 25.9 %fusion.46 = bf16[4,1,256,128]{3,2,0,1:T(8,128)(2,1)S(1)} fusion(f32[4,1,256,128]{3,2,0,1:T(8,128)S(1)} %fusion.45, bf16[16384,128]{1,0:T(8,128)(2,1)} %all-gather.8.cloned.1.call-done, f32[4,256,16384]{2,1,0:T(8,128)} %get-tuple-element.336, f32[4,256]{1,0:T(4,128)S(1)} %get-tuple-element.337, pred[4,16384]{1,0:T(4,128)(4,1)S(1)} %iota_compare_fusion, ...), kind=kOutput, calls=%fused_computation.48 | convolution fusion | flops 4379246592 | bytes 72163328 | tf_op jit(solution)/shard_map/rhqk,khd->rhqd/dot_general | solution.py:211
  231.8 4.8 %convolution_convert_fusion = bf16[256,4096]{1,0:T(8,128)(2,1)} fusion(bf16[256,512]{1,0:T(8,128)(2,1)S(1)} %reshape_transpose_reshape.4, bf16[512,4096]{1,0:T(8,128)(2,1)} %param.25), kind=kOutput, calls=%fused_computation.36 | convolution fusion | flops 1074790400 | bytes 6553600 | tf_op jit(solution)/shard_map/dot_general | solution.py:221
  238.8 32.8 %reduce-scatter.2.cloned.1.call-done = bf16[32,4096]{1,0:T(8,128)(2,1)} async-done(((bf16[256,4096]{1,0:T(8,128)(2,1)}), bf16[32,4096]{1,0:T(8,128)(2,1)}) %reduce-scatter.2.cloned.1.call-update) | async-done | bytes 262160 | tf_op jit(solution)/shard_map/reduce_scatter | solution.py:220
  (135 shorter events, 17.4 us)
Async XLA Ops:
  7.2 84.3 %copy-start = (bf16[4096,128]{1,0:T(8,128)(2,1)S(1)}, bf16[4096,128]{1,0:T(8,128)(2,1)}, u32[]{:S(2)}) copy-start(bf16[4096,128]{1,0:T(8,128)(2,1)} %param.23) | copy-start | bytes 3145732
  7.2 34.1 %all-gather.4.cloned.1.call-start = ((), (), s32[]{:S(2)}) async-start(), calls=%async_computation.1 | async-start | bytes 2359296 | tf_op jit(solution)/shard_map/all_gather | solution.py:144
  10.2 114.3 %all-gather.6.cloned.1.call-start = ((), (), s32[]{:S(2)}) async-start(), calls=%async_computation.2 | async-start | bytes 4325376 | tf_op jit(solution)/shard_map/all_gather | solution.py:196
  11.0 194.7 %all-gather.8.cloned.1.call-start = ((), (), s32[]{:S(2)}) async-start(), calls=%async_computation.3 | async-start | bytes 4325376 | tf_op jit(solution)/shard_map/all_gather | solution.py:197
  11.7 259.8 %reduce-scatter.2.cloned.1.call-start = ((), (), s32[]{:S(2)}) async-start(), calls=%async_computation.4 | async-start | bytes 2359296 | tf_op jit(solution)/shard_map/reduce_scatter | solution.py:220
  46.0 0.9 copy-start.2
  46.0 0.9 copy-start.4
  46.9 44.6 %copy-start.1 = (bf16[256,4096]{1,0:T(8,128)(2,1)S(1)}, bf16[256,4096]{1,0:T(8,128)(2,1)}, u32[]{:S(2)}) copy-start(bf16[256,4096]{1,0:T(8,128)(2,1)} %all-gather.4.cloned.1.call-done) | copy-start | bytes 6291460
  91.5 7.7 %copy-start.11 = (f32[4,1,256]{2,1,0:T(1,128)}, f32[4,1,256]{2,1,0:T(1,128)S(1)}, u32[]{:S(2)}) copy-start(f32[4,1,256]{2,1,0:T(1,128)S(1)} %get-tuple-element.269) | copy-start | bytes 12292
  91.5 33.1 %copy-start.3 = (bf16[256,4,64]{2,1,0:T(4,128)(2,1)S(1)}, bf16[256,4,64]{2,1,0:T(4,128)(2,1)}, u32[]{:S(2)}) copy-start(bf16[256,4,64]{2,1,0:T(4,128)(2,1)} %copy-done.2) | copy-start | bytes 393220
  97.2 0.6 copy-start.7
  99.2 0.7 copy-start.5
  151.8 24.4 %copy-start.12 = (f32[4,1,256]{2,1,0:T(1,128)S(1)}, f32[4,1,256]{2,1,0:T(1,128)}, u32[]{:S(2)}) copy-start(f32[4,1,256]{2,1,0:T(1,128)} %copy-done.11) | copy-start | bytes 12292
  151.8 24.5 %copy-start.6 = (f32[4,256,64]{1,2,0:T(8,128)S(1)}, f32[4,256,64]{1,2,0:T(8,128)}, u32[]{:S(2)}) copy-start(f32[4,256,64]{1,2,0:T(8,128)} %copy-done.5) | copy-start | bytes 786436
  151.8 24.4 %copy-start.9 = (bf16[256,128]{1,0:T(8,128)(2,1)S(1)}, bf16[256,128]{1,0:T(8,128)(2,1)}, u32[]{:S(2)}) copy-start(bf16[256,128]{1,0:T(8,128)(2,1)} %convolution_convert_fusion.1) | copy-start | bytes 196612
  151.8 24.4 %copy-start.10 = (f32[4,1,256,128]{3,2,1,0:T(8,128)S(1)}, f32[4,1,256,128]{3,2,1,0:T(8,128)}, u32[]{:S(2)}) copy-start(f32[4,1,256,128]{3,2,1,0:T(8,128)} %get-tuple-element.268) | copy-start | bytes 1572868
  231.8 4.9 %copy-start.13 = (s32[4,8]{1,0:T(4,128)S(1)}, s32[4,8]{1,0:T(4,128)}, u32[]{:S(2)}) copy-start(s32[4,8]{1,0:T(4,128)} %param.33) | copy-start | bytes 388
  231.8 5.6 %copy-start.8 = (bf16[4,64,128]{2,1,0:T(8,128)(2,1)S(1)}, bf16[4,64,128]{2,1,0:T(8,128)(2,1)}, u32[]{:S(2)}) copy-start(bf16[4,64,128]{2,1,0:T(8,128)(2,1)} %copy-done.7) | copy-start | bytes 196612
Sparse Core Ops, SparseCore 0:
  10.4 30.7 all-gather.3
  43.8 80.6 all-gather.5
  127.1 78.5 all-gather.7
  236.7 34.7 reduce-scatter.1
where the time goes:
time: 279 us; the launch traced here: 278 us
  waiting for transfers between devices  108 us (39%)
  matrix products  87.9 us (32%)
  other arithmetic  35.8 us (13%)
  local copies, waits for them, and re-layouts  17.8 us (6%)
  loops' own time  14.5 us (5%)
  between operations  14.2 us (5%)
    reduce_scatter x1, waiting for transfers between devices, body(): lax.psum_scatter(jnp.dot(attended, w_out, preferred_element_type=jnp.floa...  32.8 us
    all_gather x1, waiting for transfers between devices, body(): piece_values = lax.all_gather(prefix_values, 'batch', axis=0, tiled=True)  28.4 us
    dot_general x1, matrix products, body(): jnp.einsum('rhqd,khd->rhqk', queries, shaped_keys, preferred_element_type...  27.2 us
    dot_general x1, matrix products, body(): jnp.einsum('rhqk,khd->rhqd', rounded, shaped_values, preferred_element_ty...  25.9 us
    reduce_sum x9, other arithmetic, absorb(): new_sum = running_sum * factor + jnp.sum(weights, axis=-1)  25.5 us
    all_gather x1, waiting for transfers between devices, body(): piece = lax.all_gather(normed, 'tensor', axis=0, tiled=True)  23.1 us
    all_gather x1, waiting for transfers between devices, body(): piece_keys = lax.all_gather(prefix_keys, 'batch', axis=0, tiled=True)  22 us
    dot_general x7, matrix products, block_step(): jnp.einsum('hqk,khd->hqd', rounded, block_values, preferred_element_type=...  9.34 us
  transfers between devices with their start and end apart: 4, of which 4 were waited for; matrix products, arithmetic and copies ran while one was open for 38% of the time, Pallas kernels for 0%

commit v1 on v0

--- a/solution.py
+++ b/solution.py
@@ -6,6 +6,22 @@
 HD = 128
 NEG_FILL = -1e30
 HIGHEST = lax.Precision.HIGHEST
+
+
+def ring_gather(x, axis, dim):
+    ways, here, step = (lax.axis_size(axis), lax.axis_index(axis), x.shape[dim])
+    shape = [n * ways if d == dim else n for d, n in enumerate(x.shape)]
+    full = lax.dynamic_update_slice_in_dim(jnp.zeros(shape, x.dtype), x, here * step, axis=dim)
+    going_up = going_down = x
+    for far in range(1, ways // 2 + 1):
+        going_up = lax.ppermute(going_up, axis, [(d, (d + 1) % ways) for d in range(ways)])
+        full = lax.dynamic_update_slice_in_dim(full, going_up, (here - far) % ways * step, axis=dim)
+        if 2 * far < ways:
+            going_down = lax.ppermute(going_down, axis, [(d, (d - 1) % ways) for d in range(ways)])
+            full = lax.dynamic_update_slice_in_dim(
+                full, going_down, (here + far) % ways * step, axis=dim
+            )
+    return full
 
 
 def rms_normed(tokens, norm_gain):
@@ -141,7 +157,7 @@
     query_rows = tree_size * group_size
     score_scale = head_size ** (-0.5)
     normed = rms_normed(tokens, norm_gain)
-    piece = lax.all_gather(normed, "tensor", axis=0, tiled=True)
+    piece = ring_gather(normed, "tensor", 0)
     projected = jnp.concatenate(
         [
             jnp.dot(piece, w_query, preferred_element_type=jnp.float32),

time: 279 us -> 252 us (0.903)
  waiting for transfers between devices: 108 us -> 61.3 us
  starting transfers between devices: 0.16 us -> 8.99 us
  local copies, waits for them, and re-layouts: 17.8 us -> 26.5 us
    all_gather x1 -> x0, waiting for transfers between devices: 23.1 us -> none  [body(): piece = lax.all_gather(normed, 'tensor', axis=0, tiled=True)]
    all_gather x1, waiting for transfers between devices: 22 us -> 0.02 us  [body(): piece_keys = lax.all_gather(prefix_keys, 'batch', axis=0, tiled=True)]
    all_gather x1, waiting for transfers between devices: 28.4 us -> 11.3 us  [body(): piece_values = lax.all_gather(prefix_values, 'batch', axis=0, tiled=True)]
    ppermute x0 -> x7, waiting for transfers between devices: none -> 13.2 us  [the longest x4 13.2 us: ring_gather(): lax.ppermute(going_up, axis, [(d, (d + 1) % ways) for d in range(ways)])]
    ppermute x0 -> x7, starting transfers between devices: none -> 8.87 us  [the longest x3 8.86 us: ring_gather(): lax.ppermute(going_down, axis, [(d, (d - 1) % ways) for d in range(ways)])]
    dynamic_slice x8, local copies, waits for them, and re-layouts: 4.93 us -> 10.1 us  [cache_partials(): return lax.map(one_request, (queries, lower_slot, upper_slot))]
    reduce_scatter x1, waiting for transfers between devices: 32.8 us -> 36 us  [body(): lax.psum_scatter(jnp.dot(attended, w_out, preferred_element_type=jnp.floa...]
  transfers between devices with their start and end apart: 4 -> 10, of which waited for: 4 -> 5; matrix products, arithmetic and copies ran while one was open for 38% -> 48% of each run, Pallas kernels for 0% -> 0%
where the time goes in v1:
time: 252 us; the launch traced here: 251 us
  matrix products  87.1 us (35%)
  waiting for transfers between devices  61.3 us (24%)
  other arithmetic  38.2 us (15%)
  local copies, waits for them, and re-layouts  26.5 us (11%)
  loops' own time  14.3 us (6%)
  between operations  14.3 us (6%)
  starting transfers between devices  8.99 us (4%)
    reduce_scatter x1, waiting for transfers between devices, body(): lax.psum_scatter(jnp.dot(attended, w_out, preferred_element_type=jnp.floa...  36 us
    dot_general x1, matrix products, body(): jnp.einsum('rhqd,khd->rhqk', queries, shaped_keys, preferred_element_type...  27.1 us
    reduce_sum x9, other arithmetic, absorb(): new_sum = running_sum * factor + jnp.sum(weights, axis=-1)  26.4 us
    dot_general x1, matrix products, body(): jnp.einsum('rhqk,khd->rhqd', rounded, shaped_values, preferred_element_ty...  25.9 us
    ppermute x4, waiting for transfers between devices, ring_gather(): lax.ppermute(going_up, axis, [(d, (d + 1) % ways) for d in range(ways)])  13.2 us
    all_gather x1, waiting for transfers between devices, body(): piece_values = lax.all_gather(prefix_values, 'batch', axis=0, tiled=True)  11.3 us
    dynamic_slice x8, local copies, waits for them, and re-layouts, cache_partials(): return lax.map(one_request, (queries, lower_slot, upper_slot))  10.1 us
    dot_general x7, matrix products, block_step(): jnp.einsum('hqk,khd->hqd', rounded, block_values, preferred_element_type=...  9.36 us
  transfers between devices with their start and end apart: 10, of which 5 were waited for; matrix products, arithmetic and copies ran while one was open for 48% of the time, Pallas kernels for 0%

profile of v1, /device:TPU:4, one launch (start us, length us, event | category | flops | bytes accessed | tf_op | source)
XLA Modules:
  0.0 250.6 jit_solution(16129968212883265237)
XLA Ops:
  8.0 1.1 fusion.52
  9.4 1.8 constant_dynamic-update-slice_fusion.7
  11.2 3.0 %collective-permute-start.1 = (bf16[32,4096]{1,0:T(8,128)(2,1)}, bf16[32,4096]{1,0:T(8,128)(2,1)}, u32[]{:S(2)}, u32[]{:S(2)}) collective-permute-start(bf16[32,4096]{1,0:T(8,128)(2,1)} %get-tuple-element.313), channel_id=1, source_target_pairs={{0,7},{1,0},{2,1},{3,2},{4,3},{5,4},{6,5},{7,6},{8,15},{9,8},{10,9... | collective-permute-start | bytes 786440 | tf_op jit(solution)/shard_map/ppermute | solution.py:20
  14.2 1.0 convolution_minimum_fusion.6
  17.9 1.3 bitcast_subtract_fusion
  20.0 1.2 multiply_cosine_fusion
  21.2 3.0 %collective-permute-start.3 = (bf16[32,4096]{1,0:T(8,128)(2,1)}, bf16[32,4096]{1,0:T(8,128)(2,1)S(1)}, u32[]{:S(2)}, u32[]{:S(2)}) collective-permute-start(bf16[32,4096]{1,0:T(8,128)(2,1)} %collective-permute-done.1), channel_id=1, source_target_pairs={{0,7},{1,0},{2,1},{3,2},{4,3},{5,4},{6,5},{7,6},{8,15},{9,8},{10,9... | collective-permute-start | bytes 786440 | tf_op jit(solution)/shard_map/ppermute | solution.py:20
  26.1 2.3 collective-permute-done.2
  28.4 3.0 %collective-permute-start.5 = (bf16[32,4096]{1,0:T(8,128)(2,1)S(1)}, bf16[32,4096]{1,0:T(8,128)(2,1)S(1)}, u32[]{:S(2)}, u32[]{:S(2)}) collective-permute-start(bf16[32,4096]{1,0:T(8,128)(2,1)S(1)} %collective-permute-done.3), channel_id=1, source_target_pairs={{0,7},{1,0},{2,1},{3,2},{4,3},{5,4},{6,5},{7,6},{8,15},{9,8},{10,9... | collective-permute-start | bytes 786440 | tf_op jit(solution)/shard_map/ppermute | solution.py:20
  31.4 4.0 %collective-permute-done.4 = bf16[32,4096]{1,0:T(8,128)(2,1)S(1)} collective-permute-done((bf16[32,4096]{1,0:T(8,128)(2,1)S(1)}, bf16[32,4096]{1,0:T(8,128)(2,1)S(1)}, u32[]{:S(2)}, u32[]{:S(2)}) %collective-permute-start.4) | collective-permute-done | bytes 262176 | tf_op jit(solution)/shard_map/ppermute | solution.py:17
  35.4 6.9 %collective-permute-done.6 = bf16[32,4096]{1,0:T(8,128)(2,1)S(1)} collective-permute-done((bf16[32,4096]{1,0:T(8,128)(2,1)S(1)}, bf16[32,4096]{1,0:T(8,128)(2,1)S(1)}, u32[]{:S(2)}, u32[]{:S(2)}) %collective-permute-start.6) | collective-permute-done | bytes 262176 | tf_op jit(solution)/shard_map/ppermute | solution.py:17
  44.4 4.2 %fusion.86 = f32[256,512]{1,0:T(8,128)} fusion(bf16[256,4096]{1,0:T(8,128)(2,1)S(1)} %constant_dynamic-update-slice_fusion, bf16[4096,512]{1,0:T(8,128)(2,1)} %param.22), kind=kOutput, calls=%fused_computation.141 | convolution fusion | flops 1073741824 | bytes 6815744 | tf_op jit(solution)/shard_map/dot_general | solution.py:163
  48.7 2.0 reshape.401
  51.6 1.7 subtract_convert_fusion
  56.4 51.8 %while.69 = (s32[]{:T(128)}, f32[4,1,256]{2,1,0:T(1,128)S(1)}, f32[4,1,256]{2,1,0:T(1,128)}, f32[4,1,256,128]{3,2,1,0:T(8,128)}, s32[4]{0:T(128)}, /*index=5*/s3...) while((s32[]{:T(128)}, f32[4,1,256]{2,1,0:T(1,128)S(1)}, ...), condition=%wide.region_9.10_spmd, body=%wide.region_4.0_spmd.sunk | while | flops 68356632 | bytes 2713316 | solution.py:132
  56.4 1.3 dynamic_slice.58
  57.7 1.3 dynamic_slice.59
  61.1 4.0 %while.70 = (s32[]{:T(128)}, f32[1,256]{1,0:T(1,128)S(1)}, f32[1,256]{1,0:T(1,128)S(1)}, f32[1,256,128]{2,1,0:T(8,128)S(1)}, s32[]{:T(128)}, /*index=5*/s32[]{:T...) while((s32[]{:T(128)}, f32[1,256]{1,0:T(1,128)S(1)}, ...), condition=%wide.region_8.8_spmd, body=%wide.region_5.7_spmd.sunk | while | flops 68356616 | bytes 2181345 | solution.py:130
  62.4 1.2 fusion.118
  63.8 1.3 fusion.120
  66.4 1.3 dynamic_slice.58
  67.6 1.3 dynamic_slice.59
  71.1 16.0 %while.70 = (s32[]{:T(128)}, f32[1,256]{1,0:T(1,128)S(1)}, f32[1,256]{1,0:T(1,128)S(1)}, f32[1,256,128]{2,1,0:T(8,128)S(1)}, s32[]{:T(128)}, /*index=5*/s32[]{:T...) while((s32[]{:T(128)}, f32[1,256]{1,0:T(1,128)S(1)}, ...), condition=%wide.region_8.8_spmd, body=%wide.region_5.7_spmd.sunk | while | flops 68356616 | bytes 2181345 | solution.py:130
  72.4 1.2 fusion.118
  73.7 1.3 fusion.120
  76.4 1.2 fusion.118
  77.7 1.3 fusion.120
  80.4 1.2 fusion.118
  81.7 1.3 fusion.120
  84.4 1.2 fusion.118
  85.7 1.3 fusion.120
  88.3 1.3 dynamic_slice.58
  89.6 1.3 dynamic_slice.59
  93.0 4.0 %while.70 = (s32[]{:T(128)}, f32[1,256]{1,0:T(1,128)S(1)}, f32[1,256]{1,0:T(1,128)S(1)}, f32[1,256,128]{2,1,0:T(8,128)S(1)}, s32[]{:T(128)}, /*index=5*/s32[]{:T...) while((s32[]{:T(128)}, f32[1,256]{1,0:T(1,128)S(1)}, ...), condition=%wide.region_8.8_spmd, body=%wide.region_5.7_spmd.sunk | while | flops 68356616 | bytes 2181345 | solution.py:130
  94.3 1.2 fusion.118
  95.7 1.3 fusion.120
  98.3 1.3 dynamic_slice.58
  99.6 1.3 dynamic_slice.59
  103.0 4.0 %while.70 = (s32[]{:T(128)}, f32[1,256]{1,0:T(1,128)S(1)}, f32[1,256]{1,0:T(1,128)S(1)}, f32[1,256,128]{2,1,0:T(8,128)S(1)}, s32[]{:T(128)}, /*index=5*/s32[]{:T...) while((s32[]{:T(128)}, f32[1,256]{1,0:T(1,128)S(1)}, ...), condition=%wide.region_8.8_spmd, body=%wide.region_5.7_spmd.sunk | while | flops 68356616 | bytes 2181345 | solution.py:130
  104.3 1.2 fusion.118
  105.6 1.3 fusion.120
  108.2 1.9 convolution_convert_fusion.1
  111.2 27.1 %fusion.17 = (f32[4,256]{1,0:T(4,128)S(1)}, f32[4,256,16384]{2,1,0:T(8,128)}) fusion(pred[4,16384]{1,0:T(4,128)(4,1)S(1)} %iota_compare_fusion, bf16[16384,128]{1,0:T(8,128)(2,1)} %all-gather.3.cloned.1.call-done, bf16[4,256,64]{2,1,0:T(8,128)(2,1)} %bitcast.194, bf16[4,256,64]{2,1,0:T(8,128)(2,1)} %bitcast.191), kind=kOutput, calls=%fused_computation.30 | convolution fusion | flops 4345822208 | bytes 71634944 | tf_op jit(solution)/shard_map/rhqd,khd->rhqk/dot_general | solution.py:220
  138.4 24.2 %fusion.18 = f32[4,256]{1,0:T(4,128)S(1)} fusion(f32[4,256,16384]{2,1,0:T(8,128)} %get-tuple-element.338, f32[4,256]{1,0:T(4,128)S(1)} %get-tuple-element.339, pred[4,16384]{1,0:T(4,128)(4,1)S(1)} %iota_compare_fusion), kind=kLoop, calls=%fused_computation.31 | loop fusion | flops 83885056 | bytes 67182592 | tf_op jit(solution)/shard_map/reduce_sum | solution.py:69
  163.8 11.3 %all-gather.5.cloned.1.call-done = bf16[16384,128]{1,0:T(8,128)(2,1)} async-done(((bf16[512,128]{1,0:T(8,128)(2,1)}), bf16[16384,128]{1,0:T(8,128)(2,1)}) %all-gather.5.cloned.1.call-update) | async-done | bytes 4194320 | tf_op jit(solution)/shard_map/all_gather | solution.py:213
  175.1 25.9 %fusion.46 = bf16[4,1,256,128]{3,2,0,1:T(8,128)(2,1)S(1)} fusion(f32[4,1,256,128]{3,2,0,1:T(8,128)S(1)} %fusion.45, bf16[16384,128]{1,0:T(8,128)(2,1)} %all-gather.5.cloned.1.call-done, f32[4,256,16384]{2,1,0:T(8,128)} %get-tuple-element.338, f32[4,256]{1,0:T(4,128)S(1)} %get-tuple-element.339, pred[4,16384]{1,0:T(4,128)(4,1)S(1)} %iota_compare_fusion, ...), kind=kOutput, calls=%fused_computation.48 | convolution fusion | flops 4379246592 | bytes 72163328 | tf_op jit(solution)/shard_map/rhqk,khd->rhqd/dot_general | solution.py:227
  201.1 4.8 %convolution_convert_fusion = bf16[256,4096]{1,0:T(8,128)(2,1)} fusion(bf16[256,512]{1,0:T(8,128)(2,1)S(1)} %reshape_transpose_reshape.4, bf16[512,4096]{1,0:T(8,128)(2,1)} %param.25), kind=kOutput, calls=%fused_computation.36 | convolution fusion | flops 1074790400 | bytes 6553600 | tf_op jit(solution)/shard_map/dot_general | solution.py:237
  208.1 36.0 %reduce-scatter.2.cloned.1.call-done = bf16[32,4096]{1,0:T(8,128)(2,1)} async-done(((bf16[256,4096]{1,0:T(8,128)(2,1)}), bf16[32,4096]{1,0:T(8,128)(2,1)}) %reduce-scatter.2.cloned.1.call-update) | async-done | bytes 262160 | tf_op jit(solution)/shard_map/reduce_scatter | solution.py:236
  (146 shorter events, 26.6 us)
Async XLA Ops:
  7.2 35.2 %copy-start = (bf16[4096,128]{1,0:T(8,128)(2,1)S(1)}, bf16[4096,128]{1,0:T(8,128)(2,1)}, u32[]{:S(2)}) copy-start(bf16[4096,128]{1,0:T(8,128)(2,1)} %param.23) | copy-start | bytes 3145732
  7.2 9.8 %copy-start.8 = (s32[4]{0:T(128)S(1)}, s32[4]{0:T(128)}, u32[]{:S(2)}) copy-start(s32[4]{0:T(128)} %param.31) | copy-start | bytes 52
  7.2 9.9 %copy-start.9 = (s32[128]{0:T(128)S(1)}, s32[128]{0:T(128)}, u32[]{:S(2)}) copy-start(s32[128]{0:T(128)} %param.30) | copy-start | bytes 1540
  7.2 104.0 %all-gather.3.cloned.1.call-start = ((), (), s32[]{:S(2)}) async-start(), calls=%async_computation.1 | async-start | bytes 4325376 | tf_op jit(solution)/shard_map/all_gather | solution.py:212
  7.9 167.1 %all-gather.5.cloned.1.call-start = ((), (), s32[]{:S(2)}) async-start(), calls=%async_computation.2 | async-start | bytes 4325376 | tf_op jit(solution)/shard_map/all_gather | solution.py:213
  11.2 10.0 %collective-permute-start = (bf16[32,4096]{1,0:T(8,128)(2,1)}, bf16[32,4096]{1,0:T(8,128)(2,1)}, u32[]{:S(2)}, u32[]{:S(2)}) collective-permute-start(bf16[32,4096]{1,0:T(8,128)(2,1)} %get-tuple-element.313), channel_id=1, source_target_pairs={{0,1},{1,2},{2,3},{3,4},{4,5},{5,6},{6,7},{7,0},{8,9},{9,10},{10,1... | collective-permute-start | bytes 786440 | tf_op jit(solution)/shard_map/ppermute | solution.py:17
  11.2 10.0 %collective-permute-start.1 = (bf16[32,4096]{1,0:T(8,128)(2,1)}, bf16[32,4096]{1,0:T(8,128)(2,1)}, u32[]{:S(2)}, u32[]{:S(2)}) collective-permute-start(bf16[32,4096]{1,0:T(8,128)(2,1)} %get-tuple-element.313), channel_id=1, source_target_pairs={{0,7},{1,0},{2,1},{3,2},{4,3},{5,4},{6,5},{7,6},{8,15},{9,8},{10,9... | collective-permute-start | bytes 786440 | tf_op jit(solution)/shard_map/ppermute | solution.py:20
  14.1 230.0 %reduce-scatter.2.cloned.1.call-start = ((), (), s32[]{:S(2)}) async-start(), calls=%async_computation.3 | async-start | bytes 2359296 | tf_op jit(solution)/shard_map/reduce_scatter | solution.py:236
  21.1 7.2 %collective-permute-start.2 = (bf16[32,4096]{1,0:T(8,128)(2,1)}, bf16[32,4096]{1,0:T(8,128)(2,1)S(1)}, u32[]{:S(2)}, u32[]{:S(2)}) collective-permute-start(bf16[32,4096]{1,0:T(8,128)(2,1)} %collective-permute-done), channel_id=1, source_target_pairs={{0,1},{1,2},{2,3},{3,4},{4,5},{5,6},{6,7},{7,0},{8,9},{9,10},{10,1... | collective-permute-start | bytes 786440 | tf_op jit(solution)/shard_map/ppermute | solution.py:17
  21.2 7.2 %collective-permute-start.3 = (bf16[32,4096]{1,0:T(8,128)(2,1)}, bf16[32,4096]{1,0:T(8,128)(2,1)S(1)}, u32[]{:S(2)}, u32[]{:S(2)}) collective-permute-start(bf16[32,4096]{1,0:T(8,128)(2,1)} %collective-permute-done.1), channel_id=1, source_target_pairs={{0,7},{1,0},{2,1},{3,2},{4,3},{5,4},{6,5},{7,6},{8,15},{9,8},{10,9... | collective-permute-start | bytes 786440 | tf_op jit(solution)/shard_map/ppermute | solution.py:20
  28.4 7.0 %collective-permute-start.4 = (bf16[32,4096]{1,0:T(8,128)(2,1)S(1)}, bf16[32,4096]{1,0:T(8,128)(2,1)S(1)}, u32[]{:S(2)}, u32[]{:S(2)}) collective-permute-start(bf16[32,4096]{1,0:T(8,128)(2,1)S(1)} %collective-permute-done.2), channel_id=1, source_target_pairs={{0,1},{1,2},{2,3},{3,4},{4,5},{5,6},{6,7},{7,0},{8,9},{9,10},{10,1... | collective-permute-start | bytes 786440 | tf_op jit(solution)/shard_map/ppermute | solution.py:17
  28.4 7.0 %collective-permute-start.5 = (bf16[32,4096]{1,0:T(8,128)(2,1)S(1)}, bf16[32,4096]{1,0:T(8,128)(2,1)S(1)}, u32[]{:S(2)}, u32[]{:S(2)}) collective-permute-start(bf16[32,4096]{1,0:T(8,128)(2,1)S(1)} %collective-permute-done.3), channel_id=1, source_target_pairs={{0,7},{1,0},{2,1},{3,2},{4,3},{5,4},{6,5},{7,6},{8,15},{9,8},{10,9... | collective-permute-start | bytes 786440 | tf_op jit(solution)/shard_map/ppermute | solution.py:20
  35.4 7.0 %collective-permute-start.6 = (bf16[32,4096]{1,0:T(8,128)(2,1)S(1)}, bf16[32,4096]{1,0:T(8,128)(2,1)S(1)}, u32[]{:S(2)}, u32[]{:S(2)}) collective-permute-start(bf16[32,4096]{1,0:T(8,128)(2,1)S(1)} %collective-permute-done.4), channel_id=1, source_target_pairs={{0,1},{1,2},{2,3},{3,4},{4,5},{5,6},{6,7},{7,0},{8,9},{9,10},{10,1... | collective-permute-start | bytes 786440 | tf_op jit(solution)/shard_map/ppermute | solution.py:17
  53.3 1.6 copy-start.1
  53.3 2.5 copy-start.2
  138.4 24.3 %copy-start.6 = (f32[4,1,256]{2,1,0:T(1,128)S(1)}, f32[4,1,256]{2,1,0:T(1,128)}, u32[]{:S(2)}) copy-start(f32[4,1,256]{2,1,0:T(1,128)} %get-tuple-element.269) | copy-start | bytes 12292
  138.4 24.4 %copy-start.3 = (f32[4,256,64]{1,2,0:T(8,128)S(1)}, f32[4,256,64]{1,2,0:T(8,128)}, u32[]{:S(2)}) copy-start(f32[4,256,64]{1,2,0:T(8,128)} %get-tuple-element.336) | copy-start | bytes 786436
  138.4 24.4 %copy-start.4 = (f32[4,1,256,128]{3,2,1,0:T(8,128)S(1)}, f32[4,1,256,128]{3,2,1,0:T(8,128)}, u32[]{:S(2)}) copy-start(f32[4,1,256,128]{3,2,1,0:T(8,128)} %get-tuple-element.268) | copy-start | bytes 1572868
  138.4 24.4 %copy-start.5 = (f32[4,256]{1,0:T(4,128)S(1)}, f32[4,256]{1,0:T(4,128)}, u32[]{:S(2)}) copy-start(f32[4,256]{1,0:T(4,128)} %get-tuple-element.325) | copy-start | bytes 12292
  201.1 4.8 %copy-start.7 = (s32[4,8]{1,0:T(4,128)S(1)}, s32[4,8]{1,0:T(4,128)}, u32[]{:S(2)}) copy-start(s32[4,8]{1,0:T(4,128)} %param.33) | copy-start | bytes 388
Sparse Core Ops, SparseCore 0:
  10.6 83.1 all-gather.2
  96.4 78.6 all-gather.4
  206.1 38.0 reduce-scatter.1
